TPU v7x, 256 devices: a whole 4x4x8 slice. The times are simulated.
256 devices in a mesh: blk: 32 (over y, z), rep: 8 (over x, core).
Axes of the slice: x: 4, y: 4, z: 8, core: 2. Of those that a mesh axis runs over, the one named last changes fastest.
Arguments:
- hidden_in: bfloat16 [8, 512, 2560], P('rep', 'blk'), may hold values from -6 to 6
- w_z: bfloat16 [2560, 4096], P(None, 'blk'), may hold values from -0.125 to 0.125
- w_x: bfloat16 [2560, 4096], P(None, 'blk'), may hold values from -0.125 to 0.125
- w_bc: bfloat16 [2560, 256], replicated, may hold values from -0.125 to 0.125
- w_dt: bfloat16 [2560, 64], P(None, 'blk'), may hold values from -0.125 to 0.125
- conv_x: float32 [4, 4096], P(None, 'blk'), may hold values from -3 to 3
- conv_bc: float32 [4, 256], replicated, may hold values from -3 to 3
- dt_bias: float32 [4, 64], P(None, 'blk'), may hold values from -3 to -0.5
- a_log: float32 [64], P('blk'), may hold values from -2.5 to 0.5
- d_skip: float32 [64], P('blk'), may hold values from 0.5 to 1.5
- norm_gain: float32 [4096], P('blk'), may hold values from 0.5 to 1.5
- w_out: bfloat16 [4096, 2560], P('blk'), may hold values from -0.09375 to 0.09375
- edge_x: bfloat16 [256, 3, 4096], P('rep', None, 'blk'), may hold values from -6 to 6
- edge_bc: bfloat16 [256, 3, 256], P('rep'), may hold values from -6 to 6
- pool: float32 [384, 64, 64, 128], P('rep', 'blk'), may hold values from -0.6 to 0.6
- tenant_sizes: int32 [4], replicated, may hold values from 1 to 128, 256 in all
- owner: int32 [256, 1], P('rep'), may hold values from 0 to 7; in each aligned block of 32 rows (0 to 31, 32 to 63, ...) at most 6 rows name the same one
- accepted: int32 [256], P('rep'), may hold values from 1 to 16
- prompt_len: int32 [256], P('rep'), may hold values from 1 to 11
Outputs:
- hidden_out: bfloat16 [8, 512, 2560], P('rep', 'blk')
- new_pool: float32 [384, 64, 64, 128], P('rep', 'blk')
Inputs may be any that keep to these rules, and one draw needn't show every extreme that they name: Among the requests of one group (aligned blocks of 32 requests) each owner is named at most 6 times, a bound that some block reaches. `tenant_sizes`: the sizes sum to 256.
All inputs are finite; a program needn't handle non-finite values.
Results may differ from a plain program's by a relative error of at most 0.025.
Values may be sent and summed in bfloat16 or wider, within the bound.
A program may use at most 64 MiB of HBM per device.

v0:
```python
import jax
import jax.numpy as jnp
from jax import lax
from jax.sharding import PartitionSpec as P


def convolve(edge_cells, fresh_cells, kernel, edge_mask):
    sequence = jnp.concatenate(
        [edge_cells * edge_mask[:, :, None].astype(edge_cells.dtype), fresh_cells], 1
    ).astype(jnp.float32)
    steps_count = fresh_cells.shape[1]
    summed = kernel[0] * sequence[:, 0:steps_count]
    for offset in range(1, kernel.shape[0]):
        summed = summed + kernel[offset] * sequence[:, offset : offset + steps_count]
    return jax.nn.silu(summed).astype(jnp.bfloat16)


def shards(
    hidden_in,
    w_z,
    w_x,
    w_bc,
    w_dt,
    conv_x,
    conv_bc,
    dt_bias,
    a_log,
    d_skip,
    norm_gain,
    w_out,
    edge_x,
    edge_bc,
    pool,
    tenant_sizes,
    owner,
    accepted,
    prompt_len,
):
    highest = lax.Precision.HIGHEST
    rows_in = hidden_in[0]
    local_rows = rows_in.shape[0]
    n_req = edge_x.shape[0]
    drafts = local_rows * lax.axis_size("blk") // n_req
    state_dim = w_bc.shape[1] // 2
    heads_here = w_dt.shape[1]
    inner_here = w_z.shape[1]
    head_dim = inner_here // heads_here
    slots_here = pool.shape[0]
    cap_group = slots_here // lax.axis_size("rep")
    weights_in = (w_z, w_x, w_dt, w_bc)
    block_rows = lax.all_gather(rows_in, "blk", axis=0, tiled=True)
    projected = jnp.concatenate(
        [
            jnp.dot(block_rows, weight_cols, preferred_element_type=jnp.float32)
            for weight_cols in weights_in
        ],
        1,
    ).astype(jnp.bfloat16)
    z_all = projected[:, :inner_here]
    u_all = projected[:, inner_here : 2 * inner_here]
    dt_raw = projected[:, 2 * inner_here : 2 * inner_here + heads_here]
    bc_all = projected[:, 2 * inner_here + heads_here :]
    edge_len = edge_x.shape[1]
    edge_mask = prompt_len[:, None] >= (edge_len - jnp.arange(edge_len, dtype=jnp.int32))[None, :]
    x_conv = convolve(edge_x, u_all.reshape(n_req, drafts, inner_here), conv_x, edge_mask)
    bc_conv = convolve(edge_bc, bc_all.reshape(n_req, drafts, 2 * state_dim), conv_bc, edge_mask)
    b_half = bc_conv[:, :, :state_dim]
    c_half = bc_conv[:, :, state_dim:]
    b_float = b_half.astype(jnp.float32)
    c_float = c_half.astype(jnp.float32)
    x_heads = x_conv.reshape(n_req, drafts, heads_here, head_dim).astype(jnp.float32)
    req_index = lax.axis_index("rep") * n_req + jnp.arange(n_req, dtype=jnp.int32)
    tenant_ends = jnp.cumsum(tenant_sizes)
    tenant_id = jnp.sum((req_index[:, None] >= tenant_ends[None, :-1]).astype(jnp.int32), axis=1)
    tenant_pick = (
        tenant_id[:, None] == jnp.arange(tenant_sizes.shape[0], dtype=jnp.int32)[None, :]
    ).astype(jnp.float32)
    bias_req = jnp.dot(tenant_pick, dt_bias, precision=highest)
    step_size = jax.nn.softplus(
        dt_raw.reshape(n_req, drafts, heads_here).astype(jnp.float32) + bias_req[:, None, :]
    )
    log_decay = jnp.cumsum(step_size * (-jnp.exp(a_log))[None, None, :], axis=1)
    draft_index = jnp.arange(drafts, dtype=jnp.int32)
    causal = draft_index[:, None] >= draft_index[None, :]
    scores = jnp.einsum("rtn,rsn->rts", c_float, b_float, precision=highest)
    log_gap = log_decay[:, :, None, :] - log_decay[:, None, :, :]
    weight = (
        jnp.where(causal[None, :, :, None], jnp.exp(jnp.minimum(log_gap, 0.0)), 0.0)
        * step_size[:, None, :, :]
        * scores[:, :, :, None]
    )
    y_local = (
        jnp.einsum("rtsh,rshp->rthp", weight, x_heads, precision=highest)
        + d_skip[None, None, :, None] * x_heads
    )
    pick_last = (draft_index[None, :] == accepted[:, None] - 1).astype(jnp.float32)
    log_accept = jnp.sum(pick_last[:, :, None] * log_decay, axis=1)
    keep_draft = draft_index[None, :] < accepted[:, None]
    coef = (
        jnp.where(
            keep_draft[:, :, None],
            jnp.exp(jnp.minimum(log_accept[:, None, :] - log_decay, 0.0)),
            0.0,
        )
        * step_size
    )
    carry_decay = jnp.exp(log_accept)
    decay_now = jnp.exp(log_decay)
    owner_of = owner[:, 0]
    local_index = jnp.arange(n_req, dtype=jnp.int32)
    earlier = (owner_of[None, :] == owner_of[:, None]) & (
        local_index[None, :] < local_index[:, None]
    )
    rank_within = jnp.sum(earlier.astype(jnp.int32), axis=1)
    slot_index = owner_of * cap_group + rank_within
    fetched = lax.all_to_all(
        pool.astype(jnp.bfloat16), "rep", split_axis=0, concat_axis=0, tiled=True
    ).astype(pool.dtype)
    start_state = jnp.take(fetched, slot_index, axis=0)
    y_prior = decay_now[:, :, :, None] * jnp.einsum(
        "rhpn,rtn->rthp", start_state, c_float, precision=highest
    )
    accepted_state = carry_decay[:, :, None, None] * start_state + jnp.einsum(
        "rsh,rshp,rsn->rhpn", coef, x_heads, b_float, precision=highest
    )
    buffer = jnp.zeros(pool.shape, jnp.float32).at[slot_index].set(accepted_state)
    new_pool = lax.all_to_all(
        buffer.astype(jnp.bfloat16), "rep", split_axis=0, concat_axis=0, tiled=True
    ).astype(buffer.dtype)
    y_total = (y_local + y_prior).reshape(n_req * drafts, inner_here)
    gated = y_total * jax.nn.silu(z_all.astype(jnp.float32))
    sq_total = lax.psum(jnp.sum(gated * gated, axis=1), "blk")
    inner_all = inner_here * lax.axis_size("blk")
    normed = (gated * lax.rsqrt(sq_total / inner_all + 1e-05)[:, None] * norm_gain[None, :]).astype(
        jnp.bfloat16
    )
    block_rows = normed
    mixed = lax.psum_scatter(
        jnp.dot(block_rows, w_out, preferred_element_type=jnp.float32).astype(jnp.bfloat16),
        "blk",
        scatter_dimension=0,
        tiled=True,
    )
    return (mixed[None], new_pool)


def solution(mesh):
    placed = (
        P("rep", "blk", None),
        P(None, "blk"),
        P(None, "blk"),
        P(),
        P(None, "blk"),
        P(None, "blk"),
        P(),
        P(None, "blk"),
        P("blk"),
        P("blk"),
        P("blk"),
        P("blk", None),
        P("rep", None, "blk"),
        P("rep", None, None),
        P("rep", "blk", None, None),
        P(),
        P("rep", None),
        P("rep"),
        P("rep"),
    )
    return jax.shard_map(
        shards,
        mesh=mesh,
        in_specs=placed,
        out_specs=(P("rep", "blk", None), P("rep", "blk", None, None)),
        check_vma=False,
    )
```

profile of v0, /device:TPU:2, one launch (start us, length us, event | category | flops | bytes accessed | tf_op | source)
XLA Modules:
  0.0 418.3 jit_solution(11525417549869949106)
XLA Ops:
  7.2 0.0 copy-start
  7.2 0.0 all-gather.3.cloned.1.call-start
  7.2 0.7 all-gather.3.cloned.1.call-update
  7.9 3.4 convert_element_type.82
  11.4 5.9 %all-to-all-start = ((bf16[48,2,64,128]{3,2,1,0:T(8,128)(2,1)}), bf16[48,2,64,128]{3,2,1,0:T(8,128)(2,1)S(1)}, u32[]{:S(2)}, u32[]{:S(2)}) async-start(bf16[48,2,64,128]{3,2,1,0:T(8,128)(2,1)} %convert_element_type.82), calls=%async_computation | async-start | bytes 3145728 | tf_op jit(solution)/shard_map/all_to_all | solution.py:116
  17.3 0.2 reduce-window.4
  17.5 0.2 convert_reduce_fusion
  17.7 0.5 and_bitcast_fusion
  18.3 0.1 convert_reduce_fusion.1
  18.4 0.5 copy-done.10
  18.8 0.1 compare_convert_fusion
  18.9 0.1 broadcast_multiply_fusion
  19.0 0.6 iota_compare_fusion.5
  19.5 0.1 copy.81
  19.6 0.6 copy.75
  20.3 0.2 fusion.70
  20.4 0.6 slice_bitcast_fusion.4
  21.1 0.6 fusion.75
  21.7 0.6 fusion.72
  22.3 0.7 copy_multiply_fusion
  23.0 14.5 %all-to-all-done = bf16[48,2,64,128]{3,2,1,0:T(8,128)(2,1)S(1)} async-done(((bf16[48,2,64,128]{3,2,1,0:T(8,128)(2,1)}), bf16[48,2,64,128]{3,2,1,0:T(8,128)(2,1)S(1)}, u32[]{:S(2)}, u32[]{:S(2)}) %all-to-all-start) | async-done | bytes 1572896 | tf_op jit(solution)/shard_map/all_to_all | solution.py:116
  37.5 2.1 convert_element_type.83
  39.5 2.6 gather_fusion
  42.1 50.4 %all-gather.3.cloned.1.call-done = bf16[1,512,2560]{2,1,0:T(8,128)(2,1)} async-done(((bf16[1,16,2560]{2,1,0:T(8,128)(2,1)}), bf16[1,512,2560]{2,1,0:T(8,128)(2,1)}) %all-gather.3.cloned.1.call-update) | async-done | bytes 2621456 | tf_op jit(solution)/shard_map/all_gather | solution.py:51
  92.5 2.5 fusion.32
  95.0 0.1 reshape.171
  95.1 0.1 copy.76
  95.2 0.7 broadcast_multiply_fusion.1
  95.9 0.7 copy.80
  96.6 2.7 fusion.20
  99.3 0.1 maximum_convert_fusion.1
  99.4 0.2 multiply_convert_fusion.2
  99.6 0.9 reshape.167
  100.5 1.6 copy.77
  102.0 1.7 fusion.76
  103.7 1.2 copy.78
  104.9 1.7 multiply_reduce_fusion
  106.7 1.2 copy.85
  107.9 2.6 fusion.17
  110.6 0.1 maximum_convert_fusion
  110.7 0.3 multiply_convert_fusion
  111.1 0.2 fusion.65
  111.3 0.2 copy-done.3
  111.5 0.6 fusion.16
  112.1 2.6 fusion.13
  114.8 1.1 copy.86
  115.8 2.0 reshape.170
  117.9 1.8 copy.87
  119.7 3.7 multiply_reduce_fusion.1
  123.4 72.2 %psum.7 = f32[512]{0:T(512)S(1)} all-reduce(f32[512]{0:T(512)S(1)} %get-tuple-element.16), channel_id=1, replica_groups=mesh['blk'=32,'rep'=8] {'blk'}, use_global_device_ids=true, to_apply=%region_5.6 | all-reduce | flops 512 | bytes 4096 | tf_op jit(solution)/shard_map/psum | solution.py:132
  195.6 3.6 convolution_convert_fusion
  199.2 0.0 reduce-scatter.2.cloned.1.call-update
  199.2 0.6 copy-done.26
  199.9 1.1 copy.89
  201.0 0.1 copy.88
  201.1 0.1 copy.90
  201.2 4.6 %multiply_add_fusion = f32[32,2,64,128]{3,2,1,0:T(8,128)} fusion(f32[32,2,64,128]{3,2,1,0:T(8,128)S(1)} %gather_fusion, f32[32,2]{1,0:T(8,128)S(1)} %exp.50, pred[32]{0:T(512)(128)(4,1)S(1)} %copy-done.12, f32[32,16,2]{1,2,0:T(2,128)S(1)} %copy.90, bf16[32,16,2,64]{3,2,1,0:T(2,128)(2,1)} %reshape.167, bf16[32,16,256]{2,1,0:T(8,128)(2,1)} %copy-done.2), kind=kOutput, calls=%fused_computation.11 | convolution fusion | flops 102367232 | bytes 4591904 | tf_op jit(solution)/shard_map/rsh,rshp,rsn->rhpn/dot_general | solution.py:123
  205.7 2.1 broadcast_in_dim.31
  207.8 0.1 copy-done.1
  207.9 5.3 %scatter_fusion = f32[48,2,64,128]{3,2,1,0:T(8,128)} fusion(f32[48,2,64,128]{3,2,1,0:T(8,128)} %broadcast_in_dim.31, s32[32]{0:T(128)S(1)} %bitcast.79, f32[32,2,64,128]{3,2,1,0:T(8,128)S(1)} %copy-done.1), kind=kCustom, calls=%fused_computation.1 | custom fusion | bytes 6291584 | tf_op jit(solution)/shard_map/scatter | solution.py:126
  213.2 2.3 convert_element_type.88
  215.5 24.9 %all_to_all.10 = bf16[48,2,64,128]{3,2,1,0:T(8,128)(2,1)S(1)} all-to-all(bf16[48,2,64,128]{3,2,1,0:T(8,128)(2,1)S(1)} %convert_element_type.88), channel_id=1, replica_groups=mesh['blk'=32,'rep'=8] {'rep'}, dimensions={0} | all-to-all | bytes 3145728 | tf_op jit(solution)/shard_map/all_to_all | solution.py:127
  240.4 2.0 convert_element_type.89
  242.5 169.0 %reduce-scatter.2.cloned.1.call-done = bf16[16,2560]{1,0:T(8,128)(2,1)} async-done(((bf16[512,2560]{1,0:T(8,128)(2,1)}), bf16[16,2560]{1,0:T(8,128)(2,1)}) %reduce-scatter.2.cloned.1.call-update) | async-done | bytes 81936 | tf_op jit(solution)/shard_map/reduce_scatter | solution.py:138
  (72 shorter events, 0.2 us)
Async XLA Ops:
  7.2 100.7 %copy-start = (bf16[2560,256]{1,0:T(8,128)(2,1)S(1)}, bf16[2560,256]{1,0:T(8,128)(2,1)}, u32[]{:S(2)}) copy-start(bf16[2560,256]{1,0:T(8,128)(2,1)} %param.22) | copy-start | bytes 3932164
  7.2 85.3 %all-gather.3.cloned.1.call-start = ((), (), s32[]{:S(2)}) async-start(), calls=%async_computation.4 | async-start | bytes 2703360 | tf_op jit(solution)/shard_map/all_gather | solution.py:51
  11.3 6.0 %copy-start.30 = (s32[4]{0:T(128)S(1)}, s32[4]{0:T(128)}, u32[]{:S(2)}) copy-start(s32[4]{0:T(128)} %param.34) | copy-start | bytes 52
  11.3 6.2 %copy-start.27 = (s32[32,1]{0,1:T(1,128)S(1)}, s32[32,1]{0,1:T(1,128)}, u32[]{:S(2)}) copy-start(s32[32,1]{0,1:T(1,128)} %param.35) | copy-start | bytes 388
  11.3 7.0 %copy-start.31 = (f32[2]{0:T(128)S(1)}, f32[2]{0:T(128)}, u32[]{:S(2)}) copy-start(f32[2]{0:T(128)} %param.27) | copy-start | bytes 28
  11.3 7.5 %copy-start.28 = (s32[32]{0:T(128)S(1)}, s32[32]{0:T(128)}, u32[]{:S(2)}) copy-start(s32[32]{0:T(128)} %param.37) | copy-start | bytes 388
  11.3 7.5 %copy-start.8 = (bf16[32,3,128]{2,0,1:T(8,128)(2,1)S(1)}, bf16[32,3,128]{2,0,1:T(8,128)(2,1)}, u32[]{:S(2)}) copy-start(bf16[32,3,128]{2,0,1:T(8,128)(2,1)} %param.31) | copy-start | bytes 73732
  11.4 8.9 %copy-start.25 = (s32[32]{0:T(128)S(1)}, s32[32]{0:T(128)}, u32[]{:S(2)}) copy-start(s32[32]{0:T(128)} %param.36) | copy-start | bytes 388
  11.4 8.9 %copy-start.29 = (f32[4,2]{0,1:T(2,128)S(1)}, f32[4,2]{0,1:T(2,128)}, u32[]{:S(2)}) copy-start(f32[4,2]{0,1:T(2,128)} %param.26) | copy-start | bytes 100
  11.4 9.1 %copy-start.22 = (f32[4,128]{1,0:T(4,128)S(1)}, f32[4,128]{1,0:T(4,128)}, u32[]{:S(2)}) copy-start(f32[4,128]{1,0:T(4,128)} %param.24) | copy-start | bytes 6148
  11.4 9.7 %copy-start.17 = (f32[4,256]{1,0:T(4,128)S(1)}, f32[4,256]{1,0:T(4,128)}, u32[]{:S(2)}) copy-start(f32[4,256]{1,0:T(4,128)} %param.25) | copy-start | bytes 12292
  11.4 10.8 %copy-start.6 = (bf16[32,3,256]{2,0,1:T(8,128)(2,1)S(1)}, bf16[32,3,256]{2,0,1:T(8,128)(2,1)}, u32[]{:S(2)}) copy-start(bf16[32,3,256]{2,0,1:T(8,128)(2,1)} %param.32) | copy-start | bytes 147460
  11.4 26.1 %all-to-all-start = ((bf16[48,2,64,128]{3,2,1,0:T(8,128)(2,1)}), bf16[48,2,64,128]{3,2,1,0:T(8,128)(2,1)S(1)}, u32[]{:S(2)}, u32[]{:S(2)}) async-start(bf16[48,2,64,128]{3,2,1,0:T(8,128)(2,1)} %convert_element_type.82), calls=%async_computation | async-start | bytes 3145728 | tf_op jit(solution)/shard_map/all_to_all | solution.py:116
  17.3 394.1 %reduce-scatter.2.cloned.1.call-start = ((), (), s32[]{:S(2)}) async-start(), calls=%async_computation.3 | async-start | bytes 2703360 | tf_op jit(solution)/shard_map/reduce_scatter | solution.py:138
  18.2 0.6 copy-start.10
  39.5 53.0 %copy-start.9 = (bf16[2560,2]{0,1:T(2,128)(2,1)S(1)}, bf16[2560,2]{0,1:T(2,128)(2,1)}, u32[]{:S(2)}) copy-start(bf16[2560,2]{0,1:T(2,128)(2,1)} %param.23) | copy-start | bytes 30724
  96.6 2.8 copy-start.5
  96.6 2.8 copy-start.18
  96.6 2.8 copy-start.19
  96.6 2.8 copy-start.20
  96.6 2.8 copy-start.21
  107.9 2.7 copy-start.4
  107.9 2.8 copy-start.13
  107.9 2.8 copy-start.14
  107.9 2.8 copy-start.15
  107.9 2.8 copy-start.16
  110.5 1.0 copy-start.3
  110.5 0.9 copy-start.7
  110.6 0.9 copy-start.23
  110.6 0.9 copy-start.32
  110.7 1.4 copy-start.12
  111.1 3.7 copy-start.2
  119.7 75.9 %copy-start.24 = (f32[128]{0:T(128)S(1)}, f32[128]{0:T(128)}, u32[]{:S(2)}) copy-start(f32[128]{0:T(128)} %param.29) | copy-start | bytes 1540
  199.2 0.7 copy-start.26
  205.7 2.1 copy-start.1
  205.7 2.1 copy-start.11
Sparse Core Ops, SparseCore 0:
  10.6 81.8 all-gather.2
  199.3 212.0 reduce-scatter.1
where the time goes:
time: 419 us; the launch traced here: 418 us
  waiting for transfers between devices  235 us (56%)
  blocking collectives  97.1 us (23%)
  local copies, waits for them, and re-layouts  25.3 us (6%)
  matrix products  23.3 us (6%)
  other arithmetic  17.6 us (4%)
  between operations  14.4 us (3%)
  starting transfers between devices  5.94 us (1%)
    reduce_scatter x1, waiting for transfers between devices, shards(): lax.psum_scatter(jnp.dot(block_rows, w_out, preferred_element_type=jnp.fl...  169 us
    psum x1, blocking collectives, shards(): sq_total = lax.psum(jnp.sum(gated * gated, axis=1), 'blk')  72.2 us
    all_gather x1, waiting for transfers between devices, shards(): block_rows = lax.all_gather(rows_in, 'blk', axis=0, tiled=True)  50.4 us
    all_to_all x1, blocking collectives, shards(): lax.all_to_all(buffer.astype(jnp.bfloat16), 'rep', split_axis=0, concat_a...  24.9 us
    all_to_all x1, waiting for transfers between devices, shards(): lax.all_to_all(pool.astype(jnp.bfloat16), 'rep', split_axis=0, concat_axi...  14.5 us
    dot_general x4, matrix products, shards(): jnp.dot(block_rows, weight_cols, preferred_element_type=jnp.float32)  11.5 us
  transfers between devices with their start and end apart: 3, of which 3 were waited for; matrix products, arithmetic and copies ran while one was open for 7% of the time, Pallas kernels for 0%

commit v1 on v0

--- a/solution.py
+++ b/solution.py
@@ -129,7 +129,7 @@
     ).astype(buffer.dtype)
     y_total = (y_local + y_prior).reshape(n_req * drafts, inner_here)
     gated = y_total * jax.nn.silu(z_all.astype(jnp.float32))
-    sq_total = lax.psum(jnp.sum(gated * gated, axis=1), "blk")
+    sq_total = jnp.sum(lax.all_gather(jnp.sum(gated * gated, axis=1), "blk"), 0)
     inner_all = inner_here * lax.axis_size("blk")
     normed = (gated * lax.rsqrt(sq_total / inner_all + 1e-05)[:, None] * norm_gain[None, :]).astype(
         jnp.bfloat16

time: 419 us -> 399 us (0.952)
  blocking collectives: 97.1 us -> 72.2 us
    psum x1 -> x0, blocking collectives: 72.2 us -> none  [shards(): sq_total = lax.psum(jnp.sum(gated * gated, axis=1), 'blk')]
    all_gather x0 -> x1, blocking collectives: none -> 47.3 us  [shards(): sq_total = jnp.sum(lax.all_gather(jnp.sum(gated * gated, axis=1), 'blk'), 0)]
  transfers between devices with their start and end apart: 3 -> 3, of which waited for: 3 -> 3; matrix products, arithmetic and copies ran while one was open for 7% -> 8% of each run, Pallas kernels for 0% -> 0%
where the time goes in v1:
time: 399 us; the launch traced here: 398 us
  waiting for transfers between devices  239 us (60%)
  blocking collectives  72.2 us (18%)
  local copies, waits for them, and re-layouts  25.4 us (6%)
  matrix products  23.3 us (6%)
  other arithmetic  17.7 us (4%)
  between operations  14.4 us (4%)
  starting transfers between devices  5.94 us (1%)
    reduce_scatter x1, waiting for transfers between devices, shards(): lax.psum_scatter(jnp.dot(block_rows, w_out, preferred_element_type=jnp.fl...  173 us
    all_gather x1, waiting for transfers between devices, shards(): block_rows = lax.all_gather(rows_in, 'blk', axis=0, tiled=True)  50.4 us
    all_gather x1, blocking collectives, shards(): sq_total = jnp.sum(lax.all_gather(jnp.sum(gated * gated, axis=1), 'blk'), 0)  47.3 us
    all_to_all x1, blocking collectives, shards(): lax.all_to_all(buffer.astype(jnp.bfloat16), 'rep', split_axis=0, concat_a...  25 us
    all_to_all x1, waiting for transfers between devices, shards(): lax.all_to_all(pool.astype(jnp.bfloat16), 'rep', split_axis=0, concat_axi...  14.5 us
    dot_general x4, matrix products, shards(): jnp.dot(block_rows, weight_cols, preferred_element_type=jnp.float32)  11.5 us
  transfers between devices with their start and end apart: 3, of which 3 were waited for; matrix products, arithmetic and copies ran while one was open for 8% of the time, Pallas kernels for 0%

profile of v1, /device:TPU:2, one launch (start us, length us, event | category | flops | bytes accessed | tf_op | source)
XLA Modules:
  0.0 397.6 jit_solution(3180963296703493404)
XLA Ops:
  7.2 0.0 all-gather.5.cloned.1.call-start
  7.2 0.7 all-gather.5.cloned.1.call-update
  7.9 3.4 convert_element_type.82
  11.4 5.9 %all-to-all-start = ((bf16[48,2,64,128]{3,2,1,0:T(8,128)(2,1)}), bf16[48,2,64,128]{3,2,1,0:T(8,128)(2,1)S(1)}, u32[]{:S(2)}, u32[]{:S(2)}) async-start(bf16[48,2,64,128]{3,2,1,0:T(8,128)(2,1)} %convert_element_type.82), calls=%async_computation | async-start | bytes 3145728 | tf_op jit(solution)/shard_map/all_to_all | solution.py:116
  17.3 0.2 reduce-window.4
  17.5 0.2 convert_reduce_fusion
  17.7 0.5 and_bitcast_fusion
  18.3 0.1 convert_reduce_fusion.1
  18.4 0.5 copy-done.10
  18.8 0.1 compare_convert_fusion
  18.9 0.1 broadcast_multiply_fusion
  19.0 0.6 iota_compare_fusion.5
  19.5 0.1 copy.95
  19.6 0.6 copy.89
  20.3 0.2 fusion.70
  20.4 0.6 slice_bitcast_fusion.4
  21.1 0.6 fusion.75
  21.7 0.6 fusion.72
  22.3 0.7 copy_multiply_fusion
  23.0 14.5 %all-to-all-done = bf16[48,2,64,128]{3,2,1,0:T(8,128)(2,1)S(1)} async-done(((bf16[48,2,64,128]{3,2,1,0:T(8,128)(2,1)}), bf16[48,2,64,128]{3,2,1,0:T(8,128)(2,1)S(1)}, u32[]{:S(2)}, u32[]{:S(2)}) %all-to-all-start) | async-done | bytes 1572896 | tf_op jit(solution)/shard_map/all_to_all | solution.py:116
  37.5 2.1 convert_element_type.83
  39.5 2.6 gather_fusion
  42.1 50.4 %all-gather.5.cloned.1.call-done = bf16[1,512,2560]{2,1,0:T(8,128)(2,1)} async-done(((bf16[1,16,2560]{2,1,0:T(8,128)(2,1)}), bf16[1,512,2560]{2,1,0:T(8,128)(2,1)}) %all-gather.5.cloned.1.call-update) | async-done | bytes 2621456 | tf_op jit(solution)/shard_map/all_gather | solution.py:51
  92.5 2.5 fusion.32
  95.0 0.1 reshape.175
  95.1 0.1 copy.90
  95.2 0.7 broadcast_multiply_fusion.1
  95.9 0.7 copy.94
  96.6 2.7 fusion.20
  99.3 0.1 maximum_convert_fusion.1
  99.4 0.2 multiply_convert_fusion.2
  99.6 0.9 reshape.171
  100.5 1.6 copy.91
  102.0 1.7 fusion.76
  103.7 1.2 copy.92
  104.9 1.7 multiply_reduce_fusion
  106.7 1.2 copy.99
  107.9 2.6 fusion.17
  110.6 0.1 maximum_convert_fusion
  110.7 0.3 multiply_convert_fusion
  111.1 0.2 fusion.65
  111.3 0.2 copy-done.3
  111.5 0.6 fusion.16
  112.1 2.6 fusion.13
  114.8 1.1 copy.100
  115.8 2.0 reshape.174
  117.9 1.8 copy.101
  119.7 3.7 multiply_reduce_fusion.1
  123.4 47.3 %all-gather.2 = f32[32,1,512]{2,1,0:T(1,128)S(1)} all-gather(f32[1,1,512]{2,1,0:T(1,128)S(1)} %bitcast.85), channel_id=3, replica_groups=mesh['blk'=32,'rep'=8] {'blk'}, dimensions={0}, use_global_device_ids=true | all-gather | bytes 67584 | tf_op jit(solution)/shard_map/all_gather | solution.py:132
  170.6 0.1 reduce_sum.51
  170.7 3.6 convolution_convert_fusion
  174.3 0.0 reduce-scatter.2.cloned.1.call-update
  174.4 0.6 copy-done.26
  175.0 1.1 copy.103
  176.1 0.1 copy.102
  176.2 0.1 copy.104
  176.3 4.6 %multiply_add_fusion = f32[32,2,64,128]{3,2,1,0:T(8,128)} fusion(f32[32,2,64,128]{3,2,1,0:T(8,128)S(1)} %gather_fusion, f32[32,2]{1,0:T(8,128)S(1)} %exp.50, pred[32]{0:T(512)(128)(4,1)S(1)} %copy-done.12, f32[32,16,2]{1,2,0:T(2,128)S(1)} %copy.104, bf16[32,16,2,64]{3,2,1,0:T(2,128)(2,1)} %reshape.171, bf16[32,16,256]{2,1,0:T(8,128)(2,1)} %copy-done.2), kind=kOutput, calls=%fused_computation.11 | convolution fusion | flops 102367232 | bytes 4591904 | tf_op jit(solution)/shard_map/rsh,rshp,rsn->rhpn/dot_general | solution.py:123
  180.9 2.1 broadcast_in_dim.31
  182.9 0.1 copy-done.1
  183.0 5.4 %scatter_fusion = f32[48,2,64,128]{3,2,1,0:T(8,128)} fusion(f32[48,2,64,128]{3,2,1,0:T(8,128)} %broadcast_in_dim.31, s32[32]{0:T(128)S(1)} %bitcast.80, f32[32,2,64,128]{3,2,1,0:T(8,128)S(1)} %copy-done.1), kind=kCustom, calls=%fused_computation.1 | custom fusion | bytes 6291584 | tf_op jit(solution)/shard_map/scatter | solution.py:126
  188.4 2.3 convert_element_type.88
  190.7 25.0 %all_to_all.10 = bf16[48,2,64,128]{3,2,1,0:T(8,128)(2,1)S(1)} all-to-all(bf16[48,2,64,128]{3,2,1,0:T(8,128)(2,1)S(1)} %convert_element_type.88), channel_id=1, replica_groups=mesh['blk'=32,'rep'=8] {'rep'}, dimensions={0} | all-to-all | bytes 3145728 | tf_op jit(solution)/shard_map/all_to_all | solution.py:127
  215.6 2.0 convert_element_type.89
  217.7 173.1 %reduce-scatter.2.cloned.1.call-done = bf16[16,2560]{1,0:T(8,128)(2,1)} async-done(((bf16[512,2560]{1,0:T(8,128)(2,1)}), bf16[16,2560]{1,0:T(8,128)(2,1)}) %reduce-scatter.2.cloned.1.call-update) | async-done | bytes 81936 | tf_op jit(solution)/shard_map/reduce_scatter | solution.py:138
  (73 shorter events, 0.2 us)
Async XLA Ops:
  7.2 100.7 %copy-start = (bf16[2560,256]{1,0:T(8,128)(2,1)S(1)}, bf16[2560,256]{1,0:T(8,128)(2,1)}, u32[]{:S(2)}) copy-start(bf16[2560,256]{1,0:T(8,128)(2,1)} %param.22) | copy-start | bytes 3932164
  7.2 85.3 %all-gather.5.cloned.1.call-start = ((), (), s32[]{:S(2)}) async-start(), calls=%async_computation.4 | async-start | bytes 2703360 | tf_op jit(solution)/shard_map/all_gather | solution.py:51
  11.3 6.0 %copy-start.30 = (s32[4]{0:T(128)S(1)}, s32[4]{0:T(128)}, u32[]{:S(2)}) copy-start(s32[4]{0:T(128)} %param.34) | copy-start | bytes 52
  11.3 6.2 %copy-start.27 = (s32[32,1]{0,1:T(1,128)S(1)}, s32[32,1]{0,1:T(1,128)}, u32[]{:S(2)}) copy-start(s32[32,1]{0,1:T(1,128)} %param.35) | copy-start | bytes 388
  11.3 7.0 %copy-start.31 = (f32[2]{0:T(128)S(1)}, f32[2]{0:T(128)}, u32[]{:S(2)}) copy-start(f32[2]{0:T(128)} %param.27) | copy-start | bytes 28
  11.3 7.5 %copy-start.28 = (s32[32]{0:T(128)S(1)}, s32[32]{0:T(128)}, u32[]{:S(2)}) copy-start(s32[32]{0:T(128)} %param.37) | copy-start | bytes 388
  11.3 7.5 %copy-start.8 = (bf16[32,3,128]{2,0,1:T(8,128)(2,1)S(1)}, bf16[32,3,128]{2,0,1:T(8,128)(2,1)}, u32[]{:S(2)}) copy-start(bf16[32,3,128]{2,0,1:T(8,128)(2,1)} %param.31) | copy-start | bytes 73732
  11.4 8.9 %copy-start.25 = (s32[32]{0:T(128)S(1)}, s32[32]{0:T(128)}, u32[]{:S(2)}) copy-start(s32[32]{0:T(128)} %param.36) | copy-start | bytes 388
  11.4 8.9 %copy-start.29 = (f32[4,2]{0,1:T(2,128)S(1)}, f32[4,2]{0,1:T(2,128)}, u32[]{:S(2)}) copy-start(f32[4,2]{0,1:T(2,128)} %param.26) | copy-start | bytes 100
  11.4 9.1 %copy-start.22 = (f32[4,128]{1,0:T(4,128)S(1)}, f32[4,128]{1,0:T(4,128)}, u32[]{:S(2)}) copy-start(f32[4,128]{1,0:T(4,128)} %param.24) | copy-start | bytes 6148
  11.4 9.7 %copy-start.17 = (f32[4,256]{1,0:T(4,128)S(1)}, f32[4,256]{1,0:T(4,128)}, u32[]{:S(2)}) copy-start(f32[4,256]{1,0:T(4,128)} %param.25) | copy-start | bytes 12292
  11.4 10.8 %copy-start.6 = (bf16[32,3,256]{2,0,1:T(8,128)(2,1)S(1)}, bf16[32,3,256]{2,0,1:T(8,128)(2,1)}, u32[]{:S(2)}) copy-start(bf16[32,3,256]{2,0,1:T(8,128)(2,1)} %param.32) | copy-start | bytes 147460
  11.4 26.1 %all-to-all-start = ((bf16[48,2,64,128]{3,2,1,0:T(8,128)(2,1)}), bf16[48,2,64,128]{3,2,1,0:T(8,128)(2,1)S(1)}, u32[]{:S(2)}, u32[]{:S(2)}) async-start(bf16[48,2,64,128]{3,2,1,0:T(8,128)(2,1)} %convert_element_type.82), calls=%async_computation | async-start | bytes 3145728 | tf_op jit(solution)/shard_map/all_to_all | solution.py:116
  17.3 373.5 %reduce-scatter.2.cloned.1.call-start = ((), (), s32[]{:S(2)}) async-start(), calls=%async_computation.3 | async-start | bytes 2703360 | tf_op jit(solution)/shard_map/reduce_scatter | solution.py:138
  18.2 0.6 copy-start.10
  39.5 53.0 %copy-start.9 = (bf16[2560,2]{0,1:T(2,128)(2,1)S(1)}, bf16[2560,2]{0,1:T(2,128)(2,1)}, u32[]{:S(2)}) copy-start(bf16[2560,2]{0,1:T(2,128)(2,1)} %param.23) | copy-start | bytes 30724
  96.6 2.8 copy-start.5
  96.6 2.8 copy-start.18
  96.6 2.8 copy-start.19
  96.6 2.8 copy-start.20
  96.6 2.8 copy-start.21
  107.9 2.7 copy-start.4
  107.9 2.8 copy-start.13
  107.9 2.8 copy-start.14
  107.9 2.8 copy-start.15
  107.9 2.8 copy-start.16
  110.5 1.0 copy-start.3
  110.5 0.9 copy-start.7
  110.6 0.9 copy-start.23
  110.6 0.9 copy-start.32
  110.7 1.4 copy-start.12
  111.1 3.7 copy-start.2
  119.7 51.1 %copy-start.24 = (f32[128]{0:T(128)S(1)}, f32[128]{0:T(128)}, u32[]{:S(2)}) copy-start(f32[128]{0:T(128)} %param.29) | copy-start | bytes 1540
  174.3 0.7 copy-start.26
  180.9 2.1 copy-start.1
  180.9 2.1 copy-start.11
Sparse Core Ops, SparseCore 0:
  10.6 81.8 all-gather.4
  174.5 216.2 reduce-scatter.1
